TPU v7x, 256 devices: a whole 4x4x8 slice. The times are simulated.
256 devices in a mesh: phi: 64 (over z, x, y_lo), row: 4 (over y_hi, core).
Axes of the slice: x: 4, y: 4 (y_hi: 2, y_lo: 2; y = y_hi * 2 + y_lo), z: 8, core: 2. Of those that a mesh axis runs over, the one named last changes fastest.
Arguments:
- density: float32 [1024, 32, 512], P('phi', None, 'row'), may hold values from 0.5 to 2
- velocity: float32 [3, 1024, 32, 512], P(None, 'phi', None, 'row'), may hold values from -0.3 to 0.3
- shifts: int32 [64], P('row'), may hold values from 0 to 255, as said below
- fractions: float32 [64], P('row'), may hold values from 0 to 1
Outputs:
- density_out: float32 [1024, 32, 512], P('phi', None, 'row')
- stepped_velocity: float32 [3, 1024, 32, 512], P(None, 'phi', None, 'row')
- image: float32 [1024, 1024], P(('phi', 'row'))
Inputs may be any that keep to these rules, and one draw needn't show every extreme that they name: `shifts`: some band has shift 0 and some band has shift 256 - 1.
All inputs are finite; a program needn't handle non-finite values.
Results may differ from a plain program's by a relative error of at most 0.000071.
Values sent between devices are 32-bit elements; how exact they have to be, the bound alone decides.
A program may use at most 64 MiB of HBM per device.

v0:
```python
import jax
import jax.numpy as jnp
from jax import lax
from jax.sharding import PartitionSpec as P

BAND = 8
STEPS = 2
NPIX = 1024
SPEED = 1.5
COURANT = 0.05
KAPPA = 1.5
R_INNER = 0.2


def padded(cells, sides, width, closed):
    for axis, dim in sides:
        count = lax.axis_size(axis)
        ends = count if closed else count - 1
        head = lax.slice_in_dim(cells, 0, width, axis=dim)
        tail = lax.slice_in_dim(cells, cells.shape[dim] - width, cells.shape[dim], axis=dim)
        cells = jnp.concatenate(
            [
                lax.ppermute(tail, axis, [(i, (i + 1) % count) for i in range(ends)]),
                cells,
                lax.ppermute(head, axis, [((i + 1) % count, i) for i in range(ends)]),
            ],
            axis=dim,
        )
    return cells


def passed_along(value, axis, steps):
    count = lax.axis_size(axis)
    pairs = [(source, (source + steps) % count) for source in range(count)]
    return lax.ppermute(value, axis, pairs)


def conserved(prim):
    rho = prim[0]
    return jnp.stack([rho, rho * prim[1], rho * prim[2], rho * prim[3]])


def divergence(extended, axis, comp):
    cons = conserved(extended)
    flux = cons * extended[comp][None]
    flux = flux.at[comp].add(extended[0])
    size = extended.shape[axis]
    low_c = lax.slice_in_dim(cons, 0, size - 1, axis=axis)
    high_c = lax.slice_in_dim(cons, 1, size, axis=axis)
    low_f = lax.slice_in_dim(flux, 0, size - 1, axis=axis)
    high_f = lax.slice_in_dim(flux, 1, size, axis=axis)
    face = 0.5 * (low_f + high_f) - 0.5 * SPEED * (high_c - low_c)
    return lax.slice_in_dim(face, 1, size - 1, axis=axis) - lax.slice_in_dim(
        face, 0, size - 2, axis=axis
    )


def advance(prim, ext_phi, padded_polar_grid, ext_radial):
    total = (
        divergence(ext_phi, 1, 2)
        + divergence(padded_polar_grid, 2, 3)
        + divergence(ext_radial, 3, 1)
    )
    fresh = conserved(prim) - COURANT * total
    rho = fresh[0]
    return jnp.stack([rho, fresh[1] / rho, fresh[2] / rho, fresh[3] / rho])


def column_light(rho, radial_index, total_radial):
    polar = rho.shape[1]
    dtau = KAPPA / polar * rho
    above = jnp.cumsum(dtau, axis=1) - dtau
    theta = (jnp.arange(polar, dtype=jnp.int32).astype(jnp.float32) + 0.5) / polar
    tilt = 1.0 + 0.5 * jnp.cos(jnp.pi * theta)
    radius = R_INNER + (radial_index.astype(jnp.float32) + 0.5) * (1.0 - R_INNER) / total_radial
    source = (1.0 / jnp.sqrt(radius))[None, None, :] * tilt[None, :, None]
    return jnp.sum(source * (1.0 - jnp.exp(-dtau)) * jnp.exp(-above), axis=1)


def pixel_corners(pixel_rows, npix, nphi, nrad):
    yy = ((pixel_rows.astype(jnp.float32) + 0.5) / npix * 2.0 - 1.0)[:, None]
    xx = ((jnp.arange(npix, dtype=jnp.int32).astype(jnp.float32) + 0.5) / npix * 2.0 - 1.0)[None, :]
    dist = jnp.sqrt(xx * xx + yy * yy)
    upos = (dist - R_INNER) / (1.0 - R_INNER) * nrad - 0.5
    radial_floor_index = jnp.floor(upos)
    radial_fraction = upos - radial_floor_index
    radial_lower_index = radial_floor_index.astype(jnp.int32)
    angle = jnp.arctan2(yy, xx)
    vpos = (angle + jnp.pi) / (2.0 * jnp.pi) * nphi - 0.5
    lfloor = jnp.floor(vpos)
    polar_fraction = vpos - lfloor
    polar_lower_index = lfloor.astype(jnp.int32) % nphi
    polar_upper_index = (polar_lower_index + 1) % nphi
    return [
        (polar_lower_index, radial_lower_index, (1.0 - polar_fraction) * (1.0 - radial_fraction)),
        (polar_upper_index, radial_lower_index, polar_fraction * (1.0 - radial_fraction)),
        (polar_lower_index, radial_lower_index + 1, (1.0 - polar_fraction) * radial_fraction),
        (polar_upper_index, radial_lower_index + 1, polar_fraction * radial_fraction),
    ]


def sample_block(table, corners, l_first, k_first):
    nl, nk = table.shape
    flat = table.reshape(-1)
    total = jnp.zeros(corners[0][2].shape, table.dtype)
    for lidx, kidx, weight in corners:
        lloc = lidx - l_first
        kloc = kidx - k_first
        valid = (lloc >= 0) & (lloc < nl) & (kloc >= 0) & (kloc < nk)
        spot = jnp.clip(lloc, 0, nl - 1) * nk + jnp.clip(kloc, 0, nk - 1)
        total = total + jnp.where(valid, weight * jnp.take(flat, spot), 0.0)
    return total


def body(density, velocity, shifts, fractions):
    cycle = lax.axis_size("phi")
    bands = lax.axis_size("row")
    cells = density.shape[0]
    radial = density.shape[2]
    nphi = cells * cycle
    nrad = radial * bands
    prim = jnp.concatenate([density[None], velocity], axis=0)
    shift_col = jnp.repeat(shifts, BAND)
    frac_col = jnp.repeat(fractions, BAND)
    whole = shift_col // cells
    remain = shift_col % cells
    levels = (cycle // 4 - 1).bit_length()
    for step in range(STEPS):
        ext_phi = padded(prim, (("phi", 1),), 1, True)
        ext_radial = padded(prim, (("row", 3),), 1, False)
        padded_polar_grid = jnp.pad(prim, ((0, 0), (0, 0), (1, 1), (0, 0)))
        prim = advance(prim, ext_phi, padded_polar_grid, ext_radial)
        for level in range(levels):
            moved = passed_along(prim, "phi", 2**level)
            taken = whole // 2**level % 2 == 1
            prim = jnp.where(taken[None, None, None, :], moved, prim)
        left = passed_along(prim, "phi", 1)
        joined = jnp.concatenate([left, prim], axis=1)
        lead = lax.slice_in_dim(joined, cells, 2 * cells, axis=1)
        trail = lax.slice_in_dim(joined, cells - 1, 2 * cells - 1, axis=1)
        for offset in range(1, cells):
            picked = (remain == offset)[None, None, None, :]
            lead = jnp.where(
                picked, lax.slice_in_dim(joined, cells - offset, 2 * cells - offset, axis=1), lead
            )
            trail = jnp.where(
                picked,
                lax.slice_in_dim(joined, cells - offset - 1, 2 * cells - offset - 1, axis=1),
                trail,
            )
        prim = (1.0 - frac_col) * lead + frac_col * trail
    radial_index = lax.axis_index("row") * radial + jnp.arange(radial, dtype=jnp.int32)
    intensity = column_light(prim[0], radial_index, nrad)
    rows_dev = NPIX // (cycle * bands)
    first_row = (lax.axis_index("phi") * bands + lax.axis_index("row")) * rows_dev
    pixel_rows = first_row + jnp.arange(rows_dev, dtype=jnp.int32)
    table = lax.all_gather(intensity, "row", axis=1, tiled=True)
    table = lax.all_gather(table, "phi", axis=0, tiled=True)
    image = sample_block(table, pixel_corners(pixel_rows, NPIX, nphi, nrad), 0, 0)
    return (prim[0], prim[1:], image)


def solution(mesh):
    in_specs = (P("phi", None, "row"), P(None, "phi", None, "row"), P("row"), P("row"))
    out_specs = (P("phi", None, "row"), P(None, "phi", None, "row"), P(("phi", "row"), None))
    return jax.shard_map(body, mesh=mesh, in_specs=in_specs, out_specs=out_specs, check_vma=False)
```

profile of v0, /device:TPU:16, one launch (start us, length us, event | category | flops | bytes accessed | tf_op | source)
XLA Modules:
  0.0 745.6 jit_solution(6598859238169226459)
XLA Ops:
  7.2 1.6 copy.28
  10.7 1.9 collective-permute-start.3
  13.7 2.4 collective-permute-start.2
  16.9 8.9 %collective-permute-start.1 = (f32[4,1,32,128]{3,1,2,0:T(1,128)}, f32[4,1,32,128]{3,1,2,0:T(1,128)S(1)}, u32[]{:S(2)}, u32[]{:S(2)}) collective-permute-start(f32[4,1,32,128]{3,1,2,0:T(1,128)} %get-tuple-element.146), channel_id=1, source_target_pairs={{4,0},{8,4},{12,8},{16,12},{20,16},{24,20},{28,24},{32,28},{36,32}... | collective-permute-start | bytes 196616 | tf_op jit(solution)/shard_map/ppermute | solution.py:25
  27.0 2.2 copy.37
  29.2 2.1 pad_maximum_fusion.2
  38.7 26.5 %collective-permute-done.4 = f32[4,16,32,128]{3,1,2,0:T(8,128)S(1)} collective-permute-done((f32[4,16,32,128]{3,1,2,0:T(8,128)S(1)}, f32[4,16,32,128]{3,1,2,0:T(8,128)S(1)}, u32[]{:S(2)}, u32[]{:S(2)}) %collective-permute-start.4) | collective-permute-done | bytes 1048608 | tf_op jit(solution)/shard_map/ppermute | solution.py:35
  65.4 26.2 %collective-permute-done.5 = f32[4,16,32,128]{3,1,2,0:T(8,128)S(1)} collective-permute-done((f32[4,16,32,128]{3,1,2,0:T(8,128)S(1)}, f32[4,16,32,128]{3,1,2,0:T(8,128)S(1)}, u32[]{:S(2)}, u32[]{:S(2)}) %collective-permute-start.5) | collective-permute-done | bytes 1048608 | tf_op jit(solution)/shard_map/ppermute | solution.py:35
  92.1 27.6 %collective-permute-done.6 = f32[4,16,32,128]{3,1,2,0:T(8,128)S(1)} collective-permute-done((f32[4,16,32,128]{3,1,2,0:T(8,128)S(1)}, f32[4,16,32,128]{3,1,2,0:T(8,128)S(1)}, u32[]{:S(2)}, u32[]{:S(2)}) %collective-permute-start.6) | collective-permute-done | bytes 1048608 | tf_op jit(solution)/shard_map/ppermute | solution.py:35
  119.9 17.4 %collective-permute-done.7 = f32[4,16,32,128]{3,1,2,0:T(8,128)S(1)} collective-permute-done((f32[4,16,32,128]{3,1,2,0:T(8,128)S(1)}, f32[4,16,32,128]{3,1,2,0:T(8,128)S(1)}, u32[]{:S(2)}, u32[]{:S(2)}) %collective-permute-start.7) | collective-permute-done | bytes 1048608 | tf_op jit(solution)/shard_map/ppermute | solution.py:35
  138.6 18.4 %collective-permute-done.8 = f32[4,16,32,128]{3,1,2,0:T(8,128)S(1)} collective-permute-done((f32[4,16,32,128]{3,1,2,0:T(8,128)S(1)}, f32[4,16,32,128]{3,1,2,0:T(8,128)S(1)}, u32[]{:S(2)}, u32[]{:S(2)}) %collective-permute-start.8) | collective-permute-done | bytes 1048608 | tf_op jit(solution)/shard_map/ppermute | solution.py:35
  157.2 3.5 multiply_add_fusion.1
  163.4 17.8 %collective-permute-start.12 = (f32[4,16,32,1]{2,1,3,0:T(8,128)S(1)}, f32[4,16,32,1]{2,1,3,0:T(8,128)}, u32[]{:S(2)}, u32[]{:S(2)}) collective-permute-start(f32[4,16,32,1]{2,1,3,0:T(8,128)S(1)} %copy.40), channel_id=1, source_target_pairs={{1,0},{2,1},{3,2},{5,4},{6,5},{7,6},{9,8},{10,9},{11,10},{13,12},{... | collective-permute-start | bytes 24584 | tf_op jit(solution)/shard_map/ppermute | solution.py:25
  182.3 1.9 collective-permute-start.11
  184.2 1.4 broadcast_multiply_fusion.4
  187.0 1.9 collective-permute-start.9
  188.9 1.3 copy.42
  190.7 2.2 copy.41
  192.9 2.1 pad_maximum_fusion.4
  200.7 28.2 %collective-permute-done.13 = f32[4,16,32,128]{3,1,2,0:T(8,128)S(1)} collective-permute-done((f32[4,16,32,128]{3,1,2,0:T(8,128)S(1)}, f32[4,16,32,128]{3,1,2,0:T(8,128)S(1)}, u32[]{:S(2)}, u32[]{:S(2)}) %collective-permute-start.13) | collective-permute-done | bytes 1048608 | tf_op jit(solution)/shard_map/ppermute | solution.py:35
  229.2 28.3 %collective-permute-done.14 = f32[4,16,32,128]{3,1,2,0:T(8,128)S(1)} collective-permute-done((f32[4,16,32,128]{3,1,2,0:T(8,128)S(1)}, f32[4,16,32,128]{3,1,2,0:T(8,128)S(1)}, u32[]{:S(2)}, u32[]{:S(2)}) %collective-permute-start.14) | collective-permute-done | bytes 1048608 | tf_op jit(solution)/shard_map/ppermute | solution.py:35
  257.7 26.4 %collective-permute-done.15 = f32[4,16,32,128]{3,1,2,0:T(8,128)S(1)} collective-permute-done((f32[4,16,32,128]{3,1,2,0:T(8,128)S(1)}, f32[4,16,32,128]{3,1,2,0:T(8,128)S(1)}, u32[]{:S(2)}, u32[]{:S(2)}) %collective-permute-start.15) | collective-permute-done | bytes 1048608 | tf_op jit(solution)/shard_map/ppermute | solution.py:35
  284.5 16.0 %collective-permute-done.16 = f32[4,16,32,128]{3,1,2,0:T(8,128)S(1)} collective-permute-done((f32[4,16,32,128]{3,1,2,0:T(8,128)S(1)}, f32[4,16,32,128]{3,1,2,0:T(8,128)S(1)}, u32[]{:S(2)}, u32[]{:S(2)}) %collective-permute-start.16) | collective-permute-done | bytes 1048608 | tf_op jit(solution)/shard_map/ppermute | solution.py:35
  300.9 18.9 %collective-permute-done.17 = f32[4,16,32,128]{3,1,2,0:T(8,128)S(1)} collective-permute-done((f32[4,16,32,128]{3,1,2,0:T(8,128)S(1)}, f32[4,16,32,128]{3,1,2,0:T(8,128)S(1)}, u32[]{:S(2)}, u32[]{:S(2)}) %collective-permute-start.17) | collective-permute-done | bytes 1048608 | tf_op jit(solution)/shard_map/ppermute | solution.py:35
  319.9 3.5 multiply_add_fusion
  323.6 19.1 %all_gather.6 = f32[16,512]{1,0:T(8,128)} all-gather(f32[16,128]{1,0:T(8,128)S(1)} %fusion.116), channel_id=1, replica_groups=mesh['phi'=64,'row'=4] {'row'}, dimensions={1}, use_global_device_ids=true | all-gather | bytes 40960 | tf_op jit(solution)/shard_map/all_gather | solution.py:157
  345.0 298.5 %all-gather.2.cloned.1.call-done = f32[1024,512]{1,0:T(8,128)} async-done(((f32[16,512]{1,0:T(8,128)}), f32[1024,512]{1,0:T(8,128)}) %all-gather.2.cloned.1.call-update) | async-done | bytes 2097168 | tf_op jit(solution)/shard_map/all_gather | solution.py:158
  643.5 2.1 copy.45
  645.7 23.0 %gather_fusion.3 = f32[4096]{0:T(1024)S(1)} fusion(f32[524288]{0:T(1024)S(1)} %bitcast.63, s32[4096]{0:T(1024)S(1)} %bitcast_clamp_fusion), kind=kCustom, calls=%fused_computation.3.clone | custom fusion | bytes 49152 | tf_op jit(solution)/shard_map/jit(_take)/gather | solution.py:111
  668.7 23.0 %gather_fusion.2 = f32[4096]{0:T(1024)S(1)} fusion(f32[524288]{0:T(1024)S(1)} %bitcast.64, s32[4096]{0:T(1024)S(1)} %bitcast_clamp_fusion.1), kind=kCustom, calls=%fused_computation.2.clone | custom fusion | bytes 49152 | tf_op jit(solution)/shard_map/jit(_take)/gather | solution.py:111
  691.8 23.0 %gather_fusion.1 = f32[4096]{0:T(1024)S(1)} fusion(f32[524288]{0:T(1024)S(1)} %bitcast.65, s32[4096]{0:T(1024)S(1)} %bitcast_clamp_fusion.2), kind=kCustom, calls=%fused_computation.1.clone | custom fusion | bytes 49152 | tf_op jit(solution)/shard_map/jit(_take)/gather | solution.py:111
  714.8 23.0 %gather_fusion = f32[4096]{0:T(1024)S(1)} fusion(f32[524288]{0:T(1024)S(1)} %bitcast.66, s32[4096]{0:T(1024)S(1)} %bitcast_clamp_fusion.3), kind=kCustom, calls=%fused_computation.clone | custom fusion | bytes 49152 | tf_op jit(solution)/shard_map/jit(_take)/gather | solution.py:111
  (185 shorter events, 29.9 us)
Async XLA Ops:
  7.2 636.4 %all-gather.2.cloned.1.call-start = ((), (), s32[]{:S(2)}) async-start(), calls=%async_computation | async-start | bytes 2129920 | tf_op jit(solution)/shard_map/all_gather | solution.py:158
  10.7 15.8 %collective-permute-start.3 = (f32[4,16,32,1]{2,1,3,0:T(8,128)S(1)}, f32[4,16,32,1]{2,1,3,0:T(8,128)S(1)}, u32[]{:S(2)}, u32[]{:S(2)}) collective-permute-start(f32[4,16,32,1]{2,1,3,0:T(8,128)S(1)} %copy.36), channel_id=1, source_target_pairs={{1,0},{2,1},{3,2},{5,4},{6,5},{7,6},{9,8},{10,9},{11,10},{13,12},{... | collective-permute-start | bytes 24584 | tf_op jit(solution)/shard_map/ppermute | solution.py:25
  13.7 13.3 %collective-permute-start.2 = (f32[4,16,32,1]{2,1,3,0:T(8,128)}, f32[4,16,32,1]{2,1,3,0:T(8,128)}, u32[]{:S(2)}, u32[]{:S(2)}) collective-permute-start(f32[4,16,32,1]{2,1,3,0:T(8,128)} %copy.35), channel_id=1, source_target_pairs={{0,1},{1,2},{2,3},{4,5},{5,6},{6,7},{8,9},{9,10},{10,11},{12,13},{... | collective-permute-start | bytes 24584 | tf_op jit(solution)/shard_map/ppermute | solution.py:23
  16.9 16.7 %collective-permute-start.1 = (f32[4,1,32,128]{3,1,2,0:T(1,128)}, f32[4,1,32,128]{3,1,2,0:T(1,128)S(1)}, u32[]{:S(2)}, u32[]{:S(2)}) collective-permute-start(f32[4,1,32,128]{3,1,2,0:T(1,128)} %get-tuple-element.146), channel_id=1, source_target_pairs={{4,0},{8,4},{12,8},{16,12},{20,16},{24,20},{28,24},{32,28},{36,32}... | collective-permute-start | bytes 196616 | tf_op jit(solution)/shard_map/ppermute | solution.py:25
  25.8 8.8 %collective-permute-start = (f32[4,1,32,128]{3,1,2,0:T(1,128)}, f32[4,1,32,128]{3,1,2,0:T(1,128)}, u32[]{:S(2)}, u32[]{:S(2)}) collective-permute-start(f32[4,1,32,128]{3,1,2,0:T(1,128)} %get-tuple-element.145), channel_id=1, source_target_pairs={{0,4},{4,8},{8,12},{12,16},{16,20},{20,24},{24,28},{28,32},{32,36}... | collective-permute-start | bytes 196616 | tf_op jit(solution)/shard_map/ppermute | solution.py:23
  37.9 27.3 %collective-permute-start.4 = (f32[4,16,32,128]{3,1,2,0:T(8,128)S(1)}, f32[4,16,32,128]{3,1,2,0:T(8,128)S(1)}, u32[]{:S(2)}, u32[]{:S(2)}) collective-permute-start(f32[4,16,32,128]{3,1,2,0:T(8,128)S(1)} %pad_maximum_fusion.14), channel_id=1, source_target_pairs={{0,4},{4,8},{8,12},{12,16},{16,20},{20,24},{24,28},{28,32},{32,36}... | collective-permute-start | bytes 3145736 | tf_op jit(solution)/shard_map/ppermute | solution.py:35
  38.7 81.0 %copy-start.8 = (pred[128]{0:T(512)(128)(4,1)}, pred[128]{0:T(512)(128)(4,1)S(1)}, u32[]{:S(2)}) copy-start(pred[128]{0:T(512)(128)(4,1)S(1)} %get-tuple-element.175) | copy-start | bytes 388
  65.3 26.3 %collective-permute-start.5 = (f32[4,16,32,128]{3,1,2,0:T(8,128)S(1)}, f32[4,16,32,128]{3,1,2,0:T(8,128)S(1)}, u32[]{:S(2)}, u32[]{:S(2)}) collective-permute-start(f32[4,16,32,128]{3,1,2,0:T(8,128)S(1)} %broadcast_select_fusion.1), channel_id=1, source_target_pairs={{0,8},{4,12},{8,16},{12,20},{16,24},{20,28},{24,32},{28,36},{32,40... | collective-permute-start | bytes 3145736 | tf_op jit(solution)/shard_map/ppermute | solution.py:35
  91.8 27.9 %collective-permute-start.6 = (f32[4,16,32,128]{3,1,2,0:T(8,128)S(1)}, f32[4,16,32,128]{3,1,2,0:T(8,128)S(1)}, u32[]{:S(2)}, u32[]{:S(2)}) collective-permute-start(f32[4,16,32,128]{3,1,2,0:T(8,128)S(1)} %broadcast_select_fusion.3), channel_id=1, source_target_pairs={{0,16},{4,20},{8,24},{12,28},{16,32},{20,36},{24,40},{28,44},{32,4... | collective-permute-start | bytes 3145736 | tf_op jit(solution)/shard_map/ppermute | solution.py:35
  119.8 17.5 %collective-permute-start.7 = (f32[4,16,32,128]{3,1,2,0:T(8,128)S(1)}, f32[4,16,32,128]{3,1,2,0:T(8,128)S(1)}, u32[]{:S(2)}, u32[]{:S(2)}) collective-permute-start(f32[4,16,32,128]{3,1,2,0:T(8,128)S(1)} %broadcast_select_fusion.5), channel_id=1, source_target_pairs={{0,32},{4,36},{8,40},{12,44},{16,48},{20,52},{24,56},{28,60},{32,6... | collective-permute-start | bytes 3145736 | tf_op jit(solution)/shard_map/ppermute | solution.py:35
  137.4 19.6 %collective-permute-start.8 = (f32[4,16,32,128]{3,1,2,0:T(8,128)S(1)}, f32[4,16,32,128]{3,1,2,0:T(8,128)S(1)}, u32[]{:S(2)}, u32[]{:S(2)}) collective-permute-start(f32[4,16,32,128]{3,1,2,0:T(8,128)S(1)} %broadcast_select_fusion.7), channel_id=1, source_target_pairs={{0,4},{4,8},{8,12},{12,16},{16,20},{20,24},{24,28},{28,32},{32,36}... | collective-permute-start | bytes 3145736 | tf_op jit(solution)/shard_map/ppermute | solution.py:35
  163.4 25.5 %collective-permute-start.12 = (f32[4,16,32,1]{2,1,3,0:T(8,128)S(1)}, f32[4,16,32,1]{2,1,3,0:T(8,128)}, u32[]{:S(2)}, u32[]{:S(2)}) collective-permute-start(f32[4,16,32,1]{2,1,3,0:T(8,128)S(1)} %copy.40), channel_id=1, source_target_pairs={{1,0},{2,1},{3,2},{5,4},{6,5},{7,6},{9,8},{10,9},{11,10},{13,12},{... | collective-permute-start | bytes 24584 | tf_op jit(solution)/shard_map/ppermute | solution.py:25
  182.3 8.4 %collective-permute-start.11 = (f32[4,16,32,1]{2,1,3,0:T(8,128)}, f32[4,16,32,1]{2,1,3,0:T(8,128)}, u32[]{:S(2)}, u32[]{:S(2)}) collective-permute-start(f32[4,16,32,1]{2,1,3,0:T(8,128)} %copy.39), channel_id=1, source_target_pairs={{0,1},{1,2},{2,3},{4,5},{5,6},{6,7},{8,9},{9,10},{10,11},{12,13},{... | collective-permute-start | bytes 24584 | tf_op jit(solution)/shard_map/ppermute | solution.py:23
  185.7 11.6 %collective-permute-start.10 = (f32[4,1,32,128]{3,1,2,0:T(1,128)}, f32[4,1,32,128]{3,1,2,0:T(1,128)S(1)}, u32[]{:S(2)}, u32[]{:S(2)}) collective-permute-start(f32[4,1,32,128]{3,1,2,0:T(1,128)} %get-tuple-element.130), channel_id=1, source_target_pairs={{4,0},{8,4},{12,8},{16,12},{20,16},{24,20},{28,24},{32,28},{36,32}... | collective-permute-start | bytes 196616 | tf_op jit(solution)/shard_map/ppermute | solution.py:25
  187.0 10.2 %collective-permute-start.9 = (f32[4,1,32,128]{3,1,2,0:T(1,128)}, f32[4,1,32,128]{3,1,2,0:T(1,128)}, u32[]{:S(2)}, u32[]{:S(2)}) collective-permute-start(f32[4,1,32,128]{3,1,2,0:T(1,128)} %get-tuple-element.129), channel_id=1, source_target_pairs={{0,4},{4,8},{8,12},{12,16},{16,20},{20,24},{24,28},{28,32},{32,36}... | collective-permute-start | bytes 196616 | tf_op jit(solution)/shard_map/ppermute | solution.py:23
  200.7 28.3 %collective-permute-start.13 = (f32[4,16,32,128]{3,1,2,0:T(8,128)S(1)}, f32[4,16,32,128]{3,1,2,0:T(8,128)S(1)}, u32[]{:S(2)}, u32[]{:S(2)}) collective-permute-start(f32[4,16,32,128]{3,1,2,0:T(8,128)S(1)} %pad_maximum_fusion.15), channel_id=1, source_target_pairs={{0,4},{4,8},{8,12},{12,16},{16,20},{20,24},{24,28},{28,32},{32,36}... | collective-permute-start | bytes 3145736 | tf_op jit(solution)/shard_map/ppermute | solution.py:35
  229.1 55.0 %copy-start.9 = (pred[128]{0:T(512)(128)(4,1)S(1)}, pred[128]{0:T(512)(128)(4,1)}, u32[]{:S(2)}) copy-start(pred[128]{0:T(512)(128)(4,1)} %copy-done.8) | copy-start | bytes 388
  229.1 28.4 %collective-permute-start.14 = (f32[4,16,32,128]{3,1,2,0:T(8,128)S(1)}, f32[4,16,32,128]{3,1,2,0:T(8,128)S(1)}, u32[]{:S(2)}, u32[]{:S(2)}) collective-permute-start(f32[4,16,32,128]{3,1,2,0:T(8,128)S(1)} %broadcast_select_fusion), channel_id=1, source_target_pairs={{0,8},{4,12},{8,16},{12,20},{16,24},{20,28},{24,32},{28,36},{32,40... | collective-permute-start | bytes 3145736 | tf_op jit(solution)/shard_map/ppermute | solution.py:35
  257.7 26.5 %collective-permute-start.15 = (f32[4,16,32,128]{3,1,2,0:T(8,128)S(1)}, f32[4,16,32,128]{3,1,2,0:T(8,128)S(1)}, u32[]{:S(2)}, u32[]{:S(2)}) collective-permute-start(f32[4,16,32,128]{3,1,2,0:T(8,128)S(1)} %broadcast_select_fusion.2), channel_id=1, source_target_pairs={{0,16},{4,20},{8,24},{12,28},{16,32},{20,36},{24,40},{28,44},{32,4... | collective-permute-start | bytes 3145736 | tf_op jit(solution)/shard_map/ppermute | solution.py:35
  284.3 35.5 %copy-start.7 = (f32[128]{0:T(128)S(1)}, f32[128]{0:T(128)}, u32[]{:S(2)}) copy-start(f32[128]{0:T(128)} %copy-done.6) | copy-start | bytes 1540
  284.3 35.5 %copy-start.11 = (pred[128]{0:T(512)(128)(4,1)S(1)}, pred[128]{0:T(512)(128)(4,1)}, u32[]{:S(2)}) copy-start(pred[128]{0:T(512)(128)(4,1)} %copy-done.10) | copy-start | bytes 388
  284.3 35.5 %copy-start.13 = (pred[128]{0:T(512)(128)(4,1)S(1)}, pred[128]{0:T(512)(128)(4,1)}, u32[]{:S(2)}) copy-start(pred[128]{0:T(512)(128)(4,1)} %copy-done.12) | copy-start | bytes 388
  284.3 35.5 %copy-start.15 = (pred[128]{0:T(512)(128)(4,1)S(1)}, pred[128]{0:T(512)(128)(4,1)}, u32[]{:S(2)}) copy-start(pred[128]{0:T(512)(128)(4,1)} %copy-done.14) | copy-start | bytes 388
  284.3 35.5 %copy-start.17 = (pred[128]{0:T(512)(128)(4,1)S(1)}, pred[128]{0:T(512)(128)(4,1)}, u32[]{:S(2)}) copy-start(pred[128]{0:T(512)(128)(4,1)} %copy-done.16) | copy-start | bytes 388
  284.3 35.5 %copy-start.19 = (pred[128]{0:T(512)(128)(4,1)S(1)}, pred[128]{0:T(512)(128)(4,1)}, u32[]{:S(2)}) copy-start(pred[128]{0:T(512)(128)(4,1)} %copy-done.18) | copy-start | bytes 388
  284.3 35.5 %copy-start.21 = (pred[128]{0:T(512)(128)(4,1)S(1)}, pred[128]{0:T(512)(128)(4,1)}, u32[]{:S(2)}) copy-start(pred[128]{0:T(512)(128)(4,1)} %copy-done.20) | copy-start | bytes 388
  284.3 35.5 %copy-start.23 = (pred[128]{0:T(512)(128)(4,1)S(1)}, pred[128]{0:T(512)(128)(4,1)}, u32[]{:S(2)}) copy-start(pred[128]{0:T(512)(128)(4,1)} %copy-done.22) | copy-start | bytes 388
  284.3 35.5 %copy-start.25 = (pred[128]{0:T(512)(128)(4,1)S(1)}, pred[128]{0:T(512)(128)(4,1)}, u32[]{:S(2)}) copy-start(pred[128]{0:T(512)(128)(4,1)} %copy-done.24) | copy-start | bytes 388
  284.4 35.5 %copy-start.27 = (pred[128]{0:T(512)(128)(4,1)S(1)}, pred[128]{0:T(512)(128)(4,1)}, u32[]{:S(2)}) copy-start(pred[128]{0:T(512)(128)(4,1)} %copy-done.26) | copy-start | bytes 388
  284.4 35.5 %copy-start.29 = (pred[128]{0:T(512)(128)(4,1)S(1)}, pred[128]{0:T(512)(128)(4,1)}, u32[]{:S(2)}) copy-start(pred[128]{0:T(512)(128)(4,1)} %copy-done.28) | copy-start | bytes 388
  284.4 16.1 %collective-permute-start.16 = (f32[4,16,32,128]{3,1,2,0:T(8,128)S(1)}, f32[4,16,32,128]{3,1,2,0:T(8,128)S(1)}, u32[]{:S(2)}, u32[]{:S(2)}) collective-permute-start(f32[4,16,32,128]{3,1,2,0:T(8,128)S(1)} %broadcast_select_fusion.4), channel_id=1, source_target_pairs={{0,32},{4,36},{8,40},{12,44},{16,48},{20,52},{24,56},{28,60},{32,6... | collective-permute-start | bytes 3145736 | tf_op jit(solution)/shard_map/ppermute | solution.py:35
  300.7 19.1 %collective-permute-start.17 = (f32[4,16,32,128]{3,1,2,0:T(8,128)S(1)}, f32[4,16,32,128]{3,1,2,0:T(8,128)S(1)}, u32[]{:S(2)}, u32[]{:S(2)}) collective-permute-start(f32[4,16,32,128]{3,1,2,0:T(8,128)S(1)} %broadcast_select_fusion.6), channel_id=1, source_target_pairs={{0,4},{4,8},{8,12},{12,16},{16,20},{20,24},{24,28},{28,32},{32,36}... | collective-permute-start | bytes 3145736 | tf_op jit(solution)/shard_map/ppermute | solution.py:35
  (29 other events, 483.1 us)
Sparse Core Ops, SparseCore 0:
  342.9 300.6 all-gather.1
where the time goes:
time: 746 us
  waiting for transfers between devices  534 us (72%)
  local copies, waits for them, and re-layouts  111 us (15%)
  starting transfers between devices  36.9 us (5%)
  other arithmetic  30 us (4%)
  blocking collectives  19.1 us (3%)
  between operations  15.2 us (2%)
    all_gather x1, waiting for transfers between devices, body(): table = lax.all_gather(table, 'phi', axis=0, tiled=True)  299 us
    ppermute x10, waiting for transfers between devices, passed_along(): return lax.ppermute(value, axis, pairs)  234 us
    gather x8, local copies, waits for them, and re-layouts, sample_block(): total = total + jnp.where(valid, weight * jnp.take(flat, spot), 0.0)  92.2 us
    ppermute x4, starting transfers between devices, padded(): lax.ppermute(head, axis, [((i + 1) % count, i) for i in range(ends)])  28.9 us
    all_gather x1, blocking collectives, body(): table = lax.all_gather(intensity, 'row', axis=1, tiled=True)  19.1 us
  transfers between devices with their start and end apart: 19, of which 13 were waited for; matrix products, arithmetic and copies ran while one was open for 3% of the time, Pallas kernels for 0%

commit v1 on v0

--- a/solution.py
+++ b/solution.py
@@ -155,7 +155,9 @@
     first_row = (lax.axis_index("phi") * bands + lax.axis_index("row")) * rows_dev
     pixel_rows = first_row + jnp.arange(rows_dev, dtype=jnp.int32)
     table = lax.all_gather(intensity, "row", axis=1, tiled=True)
-    table = lax.all_gather(table, "phi", axis=0, tiled=True)
+    table = jnp.concatenate(
+        lax.all_to_all(jnp.stack([table for _ in range(lax.axis_size("phi"))]), "phi", 0, 0), 0
+    )
     image = sample_block(table, pixel_corners(pixel_rows, NPIX, nphi, nrad), 0, 0)
     return (prim[0], prim[1:], image)
 

time: 746 us -> 503 us (0.67)
  the two profiles are of different devices: /device:TPU:16 before, /device:TPU:2 now
where the time goes in v1:
time: 503 us; the launch traced here: 493 us
  waiting for transfers between devices  302 us (60%)
  local copies, waits for them, and re-layouts  113 us (22%)
  starting transfers between devices  39.3 us (8%)
  other arithmetic  30 us (6%)
  blocking collectives  6.9 us (1%)
    ppermute x10, waiting for transfers between devices, passed_along(): return lax.ppermute(value, axis, pairs)  252 us
    gather x8, local copies, waits for them, and re-layouts, sample_block(): total = total + jnp.where(valid, weight * jnp.take(flat, spot), 0.0)  92.2 us
    all_to_all x1, waiting for transfers between devices, body(): lax.all_to_all(jnp.stack([table for _ in range(lax.axis_size('phi'))]), '...  49 us
    ppermute x10, starting transfers between devices, passed_along(): return lax.ppermute(value, axis, pairs)  14.8 us
  transfers between devices with their start and end apart: 19, of which 12 were waited for; matrix products, arithmetic and copies ran while one was open for 5% of the time, Pallas kernels for 0%

profile of v1, /device:TPU:2, one launch (start us, length us, event | category | flops | bytes accessed | tf_op | source)
XLA Modules:
  0.0 493.5 jit_solution(3652348346096347184)
XLA Ops:
  0.6 1.6 copy.28
  6.5 3.6 collective-permute-start.2
  10.9 1.5 collective-permute-start.1
  14.1 2.2 copy.37
  16.3 2.1 pad_maximum_fusion.2
  24.0 2.6 collective-permute-start.4
  26.8 25.0 %collective-permute-done.4 = f32[4,16,32,128]{3,1,2,0:T(8,128)S(1)} collective-permute-done((f32[4,16,32,128]{3,1,2,0:T(8,128)S(1)}, f32[4,16,32,128]{3,1,2,0:T(8,128)S(1)}, u32[]{:S(2)}, u32[]{:S(2)}) %collective-permute-start.4) | collective-permute-done | bytes 1048608 | tf_op jit(solution)/shard_map/ppermute | solution.py:35
  52.0 34.0 %collective-permute-done.5 = f32[4,16,32,128]{3,1,2,0:T(8,128)S(1)} collective-permute-done((f32[4,16,32,128]{3,1,2,0:T(8,128)S(1)}, f32[4,16,32,128]{3,1,2,0:T(8,128)S(1)}, u32[]{:S(2)}, u32[]{:S(2)}) %collective-permute-start.5) | collective-permute-done | bytes 1048608 | tf_op jit(solution)/shard_map/ppermute | solution.py:35
  86.8 27.9 %collective-permute-done.6 = f32[4,16,32,128]{3,1,2,0:T(8,128)S(1)} collective-permute-done((f32[4,16,32,128]{3,1,2,0:T(8,128)S(1)}, f32[4,16,32,128]{3,1,2,0:T(8,128)S(1)}, u32[]{:S(2)}, u32[]{:S(2)}) %collective-permute-start.6) | collective-permute-done | bytes 1048608 | tf_op jit(solution)/shard_map/ppermute | solution.py:35
  114.9 24.7 %collective-permute-done.7 = f32[4,16,32,128]{3,1,2,0:T(8,128)S(1)} collective-permute-done((f32[4,16,32,128]{3,1,2,0:T(8,128)S(1)}, f32[4,16,32,128]{3,1,2,0:T(8,128)S(1)}, u32[]{:S(2)}, u32[]{:S(2)}) %collective-permute-start.7) | collective-permute-done | bytes 1048608 | tf_op jit(solution)/shard_map/ppermute | solution.py:35
  140.6 22.7 %collective-permute-done.8 = f32[4,16,32,128]{3,1,2,0:T(8,128)S(1)} collective-permute-done((f32[4,16,32,128]{3,1,2,0:T(8,128)S(1)}, f32[4,16,32,128]{3,1,2,0:T(8,128)S(1)}, u32[]{:S(2)}, u32[]{:S(2)}) %collective-permute-start.8) | collective-permute-done | bytes 1048608 | tf_op jit(solution)/shard_map/ppermute | solution.py:35
  163.3 3.5 multiply_add_fusion.1
  172.0 3.6 collective-permute-start.11
  177.2 3.1 collective-permute-start.10
  182.8 2.2 copy.41
  185.0 2.1 pad_maximum_fusion.4
  193.5 27.8 %collective-permute-done.13 = f32[4,16,32,128]{3,1,2,0:T(8,128)S(1)} collective-permute-done((f32[4,16,32,128]{3,1,2,0:T(8,128)S(1)}, f32[4,16,32,128]{3,1,2,0:T(8,128)S(1)}, u32[]{:S(2)}, u32[]{:S(2)}) %collective-permute-start.13) | collective-permute-done | bytes 1048608 | tf_op jit(solution)/shard_map/ppermute | solution.py:35
  221.5 27.5 %collective-permute-done.14 = f32[4,16,32,128]{3,1,2,0:T(8,128)S(1)} collective-permute-done((f32[4,16,32,128]{3,1,2,0:T(8,128)S(1)}, f32[4,16,32,128]{3,1,2,0:T(8,128)S(1)}, u32[]{:S(2)}, u32[]{:S(2)}) %collective-permute-start.14) | collective-permute-done | bytes 1048608 | tf_op jit(solution)/shard_map/ppermute | solution.py:35
  249.4 27.4 %collective-permute-done.15 = f32[4,16,32,128]{3,1,2,0:T(8,128)S(1)} collective-permute-done((f32[4,16,32,128]{3,1,2,0:T(8,128)S(1)}, f32[4,16,32,128]{3,1,2,0:T(8,128)S(1)}, u32[]{:S(2)}, u32[]{:S(2)}) %collective-permute-start.15) | collective-permute-done | bytes 1048608 | tf_op jit(solution)/shard_map/ppermute | solution.py:35
  277.2 21.4 %collective-permute-done.16 = f32[4,16,32,128]{3,1,2,0:T(8,128)S(1)} collective-permute-done((f32[4,16,32,128]{3,1,2,0:T(8,128)S(1)}, f32[4,16,32,128]{3,1,2,0:T(8,128)S(1)}, u32[]{:S(2)}, u32[]{:S(2)}) %collective-permute-start.16) | collective-permute-done | bytes 1048608 | tf_op jit(solution)/shard_map/ppermute | solution.py:35
  298.8 11.0 %collective-permute-start.17 = (f32[4,16,32,128]{3,1,2,0:T(8,128)S(1)}, f32[4,16,32,128]{3,1,2,0:T(8,128)S(1)}, u32[]{:S(2)}, u32[]{:S(2)}) collective-permute-start(f32[4,16,32,128]{3,1,2,0:T(8,128)S(1)} %broadcast_select_fusion.6), channel_id=1, source_target_pairs={{0,4},{4,8},{8,12},{12,16},{16,20},{20,24},{24,28},{28,32},{32,36}... | collective-permute-start | bytes 3145736 | tf_op jit(solution)/shard_map/ppermute | solution.py:35
  310.0 13.7 %collective-permute-done.17 = f32[4,16,32,128]{3,1,2,0:T(8,128)S(1)} collective-permute-done((f32[4,16,32,128]{3,1,2,0:T(8,128)S(1)}, f32[4,16,32,128]{3,1,2,0:T(8,128)S(1)}, u32[]{:S(2)}, u32[]{:S(2)}) %collective-permute-start.17) | collective-permute-done | bytes 1048608 | tf_op jit(solution)/shard_map/ppermute | solution.py:35
  323.8 3.5 multiply_add_fusion
  327.5 6.9 %all_gather.3 = f32[16,512]{1,0:T(8,128)S(1)} all-gather(f32[16,128]{1,0:T(8,128)S(1)} %fusion.116), channel_id=1, replica_groups=mesh['phi'=64,'row'=4] {'row'}, dimensions={1}, use_global_device_ids=true | all-gather | bytes 40960 | tf_op jit(solution)/shard_map/all_gather | solution.py:157
  334.4 1.6 stack.41
  336.0 9.4 %all-to-all-start = ((f32[64,16,512]{2,1,0:T(8,128)}), f32[64,16,512]{2,1,0:T(8,128)S(1)}, u32[]{:S(2)}, u32[]{:S(2)}) async-start(f32[64,16,512]{2,1,0:T(8,128)} %stack.41), calls=%async_computation | async-start | bytes 4194304 | tf_op jit(solution)/shard_map/all_to_all | solution.py:159
  347.7 49.0 %all-to-all-done = f32[64,16,512]{2,1,0:T(8,128)S(1)} async-done(((f32[64,16,512]{2,1,0:T(8,128)}), f32[64,16,512]{2,1,0:T(8,128)S(1)}, u32[]{:S(2)}, u32[]{:S(2)}) %all-to-all-start) | async-done | bytes 2097184 | tf_op jit(solution)/shard_map/all_to_all | solution.py:159
  398.0 2.1 copy.45
  400.1 23.0 %gather_fusion.3 = f32[4096]{0:T(1024)S(1)} fusion(f32[524288]{0:T(1024)S(1)} %bitcast.63, s32[4096]{0:T(1024)S(1)} %bitcast_clamp_fusion), kind=kCustom, calls=%fused_computation.3.clone | custom fusion | bytes 49152 | tf_op jit(solution)/shard_map/jit(_take)/gather | solution.py:111
  423.2 23.0 %gather_fusion.2 = f32[4096]{0:T(1024)S(1)} fusion(f32[524288]{0:T(1024)S(1)} %bitcast.64, s32[4096]{0:T(1024)S(1)} %bitcast_clamp_fusion.1), kind=kCustom, calls=%fused_computation.2.clone | custom fusion | bytes 49152 | tf_op jit(solution)/shard_map/jit(_take)/gather | solution.py:111
  446.2 23.0 %gather_fusion.1 = f32[4096]{0:T(1024)S(1)} fusion(f32[524288]{0:T(1024)S(1)} %bitcast.65, s32[4096]{0:T(1024)S(1)} %bitcast_clamp_fusion.2), kind=kCustom, calls=%fused_computation.1.clone | custom fusion | bytes 49152 | tf_op jit(solution)/shard_map/jit(_take)/gather | solution.py:111
  469.3 23.0 %gather_fusion = f32[4096]{0:T(1024)S(1)} fusion(f32[524288]{0:T(1024)S(1)} %bitcast.66, s32[4096]{0:T(1024)S(1)} %bitcast_clamp_fusion.3), kind=kCustom, calls=%fused_computation.clone | custom fusion | bytes 49152 | tf_op jit(solution)/shard_map/jit(_take)/gather | solution.py:111
  (187 shorter events, 35.3 us)
Async XLA Ops:
  4.1 9.4 %collective-permute-start.3 = (f32[4,16,32,1]{2,1,3,0:T(8,128)S(1)}, f32[4,16,32,1]{2,1,3,0:T(8,128)S(1)}, u32[]{:S(2)}, u32[]{:S(2)}) collective-permute-start(f32[4,16,32,1]{2,1,3,0:T(8,128)S(1)} %copy.36), channel_id=1, source_target_pairs={{1,0},{2,1},{3,2},{5,4},{6,5},{7,6},{9,8},{10,9},{11,10},{13,12},{... | collective-permute-start | bytes 24584 | tf_op jit(solution)/shard_map/ppermute | solution.py:25
  6.5 7.6 %collective-permute-start.2 = (f32[4,16,32,1]{2,1,3,0:T(8,128)}, f32[4,16,32,1]{2,1,3,0:T(8,128)}, u32[]{:S(2)}, u32[]{:S(2)}) collective-permute-start(f32[4,16,32,1]{2,1,3,0:T(8,128)} %copy.35), channel_id=1, source_target_pairs={{0,1},{1,2},{2,3},{4,5},{5,6},{6,7},{8,9},{9,10},{10,11},{12,13},{... | collective-permute-start | bytes 24584 | tf_op jit(solution)/shard_map/ppermute | solution.py:23
  10.9 9.8 %collective-permute-start.1 = (f32[4,1,32,128]{3,1,2,0:T(1,128)}, f32[4,1,32,128]{3,1,2,0:T(1,128)S(1)}, u32[]{:S(2)}, u32[]{:S(2)}) collective-permute-start(f32[4,1,32,128]{3,1,2,0:T(1,128)} %get-tuple-element.146), channel_id=1, source_target_pairs={{4,0},{8,4},{12,8},{16,12},{20,16},{24,20},{28,24},{32,28},{36,32}... | collective-permute-start | bytes 196616 | tf_op jit(solution)/shard_map/ppermute | solution.py:25
  12.4 8.2 %collective-permute-start = (f32[4,1,32,128]{3,1,2,0:T(1,128)}, f32[4,1,32,128]{3,1,2,0:T(1,128)}, u32[]{:S(2)}, u32[]{:S(2)}) collective-permute-start(f32[4,1,32,128]{3,1,2,0:T(1,128)} %get-tuple-element.145), channel_id=1, source_target_pairs={{0,4},{4,8},{8,12},{12,16},{16,20},{20,24},{24,28},{28,32},{32,36}... | collective-permute-start | bytes 196616 | tf_op jit(solution)/shard_map/ppermute | solution.py:23
  24.0 27.8 %collective-permute-start.4 = (f32[4,16,32,128]{3,1,2,0:T(8,128)S(1)}, f32[4,16,32,128]{3,1,2,0:T(8,128)S(1)}, u32[]{:S(2)}, u32[]{:S(2)}) collective-permute-start(f32[4,16,32,128]{3,1,2,0:T(8,128)S(1)} %pad_maximum_fusion.14), channel_id=1, source_target_pairs={{0,4},{4,8},{8,12},{12,16},{16,20},{20,24},{24,28},{28,32},{32,36}... | collective-permute-start | bytes 3145736 | tf_op jit(solution)/shard_map/ppermute | solution.py:35
  26.8 87.9 %copy-start.9 = (pred[128]{0:T(512)(128)(4,1)}, pred[128]{0:T(512)(128)(4,1)S(1)}, u32[]{:S(2)}) copy-start(pred[128]{0:T(512)(128)(4,1)S(1)} %get-tuple-element.175) | copy-start | bytes 388
  51.9 34.1 %collective-permute-start.5 = (f32[4,16,32,128]{3,1,2,0:T(8,128)S(1)}, f32[4,16,32,128]{3,1,2,0:T(8,128)S(1)}, u32[]{:S(2)}, u32[]{:S(2)}) collective-permute-start(f32[4,16,32,128]{3,1,2,0:T(8,128)S(1)} %broadcast_select_fusion.1), channel_id=1, source_target_pairs={{0,8},{4,12},{8,16},{12,20},{16,24},{20,28},{24,32},{28,36},{32,40... | collective-permute-start | bytes 3145736 | tf_op jit(solution)/shard_map/ppermute | solution.py:35
  86.2 28.5 %collective-permute-start.6 = (f32[4,16,32,128]{3,1,2,0:T(8,128)S(1)}, f32[4,16,32,128]{3,1,2,0:T(8,128)S(1)}, u32[]{:S(2)}, u32[]{:S(2)}) collective-permute-start(f32[4,16,32,128]{3,1,2,0:T(8,128)S(1)} %broadcast_select_fusion.3), channel_id=1, source_target_pairs={{0,16},{4,20},{8,24},{12,28},{16,32},{20,36},{24,40},{28,44},{32,4... | collective-permute-start | bytes 3145736 | tf_op jit(solution)/shard_map/ppermute | solution.py:35
  114.9 24.8 %collective-permute-start.7 = (f32[4,16,32,128]{3,1,2,0:T(8,128)S(1)}, f32[4,16,32,128]{3,1,2,0:T(8,128)S(1)}, u32[]{:S(2)}, u32[]{:S(2)}) collective-permute-start(f32[4,16,32,128]{3,1,2,0:T(8,128)S(1)} %broadcast_select_fusion.5), channel_id=1, source_target_pairs={{0,32},{4,36},{8,40},{12,44},{16,48},{20,52},{24,56},{28,60},{32,6... | collective-permute-start | bytes 3145736 | tf_op jit(solution)/shard_map/ppermute | solution.py:35
  139.8 23.6 %collective-permute-start.8 = (f32[4,16,32,128]{3,1,2,0:T(8,128)S(1)}, f32[4,16,32,128]{3,1,2,0:T(8,128)S(1)}, u32[]{:S(2)}, u32[]{:S(2)}) collective-permute-start(f32[4,16,32,128]{3,1,2,0:T(8,128)S(1)} %broadcast_select_fusion.7), channel_id=1, source_target_pairs={{0,4},{4,8},{8,12},{12,16},{16,20},{20,24},{24,28},{28,32},{32,36}... | collective-permute-start | bytes 3145736 | tf_op jit(solution)/shard_map/ppermute | solution.py:35
  169.7 11.9 %collective-permute-start.12 = (f32[4,16,32,1]{2,1,3,0:T(8,128)S(1)}, f32[4,16,32,1]{2,1,3,0:T(8,128)}, u32[]{:S(2)}, u32[]{:S(2)}) collective-permute-start(f32[4,16,32,1]{2,1,3,0:T(8,128)S(1)} %copy.40), channel_id=1, source_target_pairs={{1,0},{2,1},{3,2},{5,4},{6,5},{7,6},{9,8},{10,9},{11,10},{13,12},{... | collective-permute-start | bytes 24584 | tf_op jit(solution)/shard_map/ppermute | solution.py:25
  172.0 10.8 %collective-permute-start.11 = (f32[4,16,32,1]{2,1,3,0:T(8,128)}, f32[4,16,32,1]{2,1,3,0:T(8,128)}, u32[]{:S(2)}, u32[]{:S(2)}) collective-permute-start(f32[4,16,32,1]{2,1,3,0:T(8,128)} %copy.39), channel_id=1, source_target_pairs={{0,1},{1,2},{2,3},{4,5},{5,6},{6,7},{8,9},{9,10},{10,11},{12,13},{... | collective-permute-start | bytes 24584 | tf_op jit(solution)/shard_map/ppermute | solution.py:23
  177.2 12.2 %collective-permute-start.10 = (f32[4,1,32,128]{3,1,2,0:T(1,128)}, f32[4,1,32,128]{3,1,2,0:T(1,128)S(1)}, u32[]{:S(2)}, u32[]{:S(2)}) collective-permute-start(f32[4,1,32,128]{3,1,2,0:T(1,128)} %get-tuple-element.130), channel_id=1, source_target_pairs={{4,0},{8,4},{12,8},{16,12},{20,16},{24,20},{28,24},{32,28},{36,32}... | collective-permute-start | bytes 196616 | tf_op jit(solution)/shard_map/ppermute | solution.py:25
  181.4 8.7 %collective-permute-start.9 = (f32[4,1,32,128]{3,1,2,0:T(1,128)}, f32[4,1,32,128]{3,1,2,0:T(1,128)}, u32[]{:S(2)}, u32[]{:S(2)}) collective-permute-start(f32[4,1,32,128]{3,1,2,0:T(1,128)} %get-tuple-element.129), channel_id=1, source_target_pairs={{0,4},{4,8},{8,12},{12,16},{16,20},{20,24},{24,28},{28,32},{32,36}... | collective-permute-start | bytes 196616 | tf_op jit(solution)/shard_map/ppermute | solution.py:23
  193.4 27.9 %collective-permute-start.13 = (f32[4,16,32,128]{3,1,2,0:T(8,128)S(1)}, f32[4,16,32,128]{3,1,2,0:T(8,128)S(1)}, u32[]{:S(2)}, u32[]{:S(2)}) collective-permute-start(f32[4,16,32,128]{3,1,2,0:T(8,128)S(1)} %pad_maximum_fusion.15), channel_id=1, source_target_pairs={{0,4},{4,8},{8,12},{12,16},{16,20},{20,24},{24,28},{28,32},{32,36}... | collective-permute-start | bytes 3145736 | tf_op jit(solution)/shard_map/ppermute | solution.py:35
  221.4 55.4 %copy-start.10 = (pred[128]{0:T(512)(128)(4,1)S(1)}, pred[128]{0:T(512)(128)(4,1)}, u32[]{:S(2)}) copy-start(pred[128]{0:T(512)(128)(4,1)} %copy-done.9) | copy-start | bytes 388
  221.4 27.6 %collective-permute-start.14 = (f32[4,16,32,128]{3,1,2,0:T(8,128)S(1)}, f32[4,16,32,128]{3,1,2,0:T(8,128)S(1)}, u32[]{:S(2)}, u32[]{:S(2)}) collective-permute-start(f32[4,16,32,128]{3,1,2,0:T(8,128)S(1)} %broadcast_select_fusion), channel_id=1, source_target_pairs={{0,8},{4,12},{8,16},{12,20},{16,24},{20,28},{24,32},{28,36},{32,40... | collective-permute-start | bytes 3145736 | tf_op jit(solution)/shard_map/ppermute | solution.py:35
  249.3 27.5 %collective-permute-start.15 = (f32[4,16,32,128]{3,1,2,0:T(8,128)S(1)}, f32[4,16,32,128]{3,1,2,0:T(8,128)S(1)}, u32[]{:S(2)}, u32[]{:S(2)}) collective-permute-start(f32[4,16,32,128]{3,1,2,0:T(8,128)S(1)} %broadcast_select_fusion.2), channel_id=1, source_target_pairs={{0,16},{4,20},{8,24},{12,28},{16,32},{20,36},{24,40},{28,44},{32,4... | collective-permute-start | bytes 3145736 | tf_op jit(solution)/shard_map/ppermute | solution.py:35
  277.0 46.7 %copy-start.8 = (f32[128]{0:T(128)S(1)}, f32[128]{0:T(128)}, u32[]{:S(2)}) copy-start(f32[128]{0:T(128)} %copy-done.7) | copy-start | bytes 1540
  277.0 46.7 %copy-start.12 = (pred[128]{0:T(512)(128)(4,1)S(1)}, pred[128]{0:T(512)(128)(4,1)}, u32[]{:S(2)}) copy-start(pred[128]{0:T(512)(128)(4,1)} %copy-done.11) | copy-start | bytes 388
  277.0 46.7 %copy-start.14 = (pred[128]{0:T(512)(128)(4,1)S(1)}, pred[128]{0:T(512)(128)(4,1)}, u32[]{:S(2)}) copy-start(pred[128]{0:T(512)(128)(4,1)} %copy-done.13) | copy-start | bytes 388
  277.0 46.7 %copy-start.16 = (pred[128]{0:T(512)(128)(4,1)S(1)}, pred[128]{0:T(512)(128)(4,1)}, u32[]{:S(2)}) copy-start(pred[128]{0:T(512)(128)(4,1)} %copy-done.15) | copy-start | bytes 388
  277.0 46.7 %copy-start.18 = (pred[128]{0:T(512)(128)(4,1)S(1)}, pred[128]{0:T(512)(128)(4,1)}, u32[]{:S(2)}) copy-start(pred[128]{0:T(512)(128)(4,1)} %copy-done.17) | copy-start | bytes 388
  277.0 46.7 %copy-start.20 = (pred[128]{0:T(512)(128)(4,1)S(1)}, pred[128]{0:T(512)(128)(4,1)}, u32[]{:S(2)}) copy-start(pred[128]{0:T(512)(128)(4,1)} %copy-done.19) | copy-start | bytes 388
  277.0 46.7 %copy-start.22 = (pred[128]{0:T(512)(128)(4,1)S(1)}, pred[128]{0:T(512)(128)(4,1)}, u32[]{:S(2)}) copy-start(pred[128]{0:T(512)(128)(4,1)} %copy-done.21) | copy-start | bytes 388
  277.0 46.7 %copy-start.24 = (pred[128]{0:T(512)(128)(4,1)S(1)}, pred[128]{0:T(512)(128)(4,1)}, u32[]{:S(2)}) copy-start(pred[128]{0:T(512)(128)(4,1)} %copy-done.23) | copy-start | bytes 388
  277.0 46.7 %copy-start.26 = (pred[128]{0:T(512)(128)(4,1)S(1)}, pred[128]{0:T(512)(128)(4,1)}, u32[]{:S(2)}) copy-start(pred[128]{0:T(512)(128)(4,1)} %copy-done.25) | copy-start | bytes 388
  277.0 46.7 %copy-start.28 = (pred[128]{0:T(512)(128)(4,1)S(1)}, pred[128]{0:T(512)(128)(4,1)}, u32[]{:S(2)}) copy-start(pred[128]{0:T(512)(128)(4,1)} %copy-done.27) | copy-start | bytes 388
  277.1 46.7 %copy-start.30 = (pred[128]{0:T(512)(128)(4,1)S(1)}, pred[128]{0:T(512)(128)(4,1)}, u32[]{:S(2)}) copy-start(pred[128]{0:T(512)(128)(4,1)} %copy-done.29) | copy-start | bytes 388
  277.1 21.5 %collective-permute-start.16 = (f32[4,16,32,128]{3,1,2,0:T(8,128)S(1)}, f32[4,16,32,128]{3,1,2,0:T(8,128)S(1)}, u32[]{:S(2)}, u32[]{:S(2)}) collective-permute-start(f32[4,16,32,128]{3,1,2,0:T(8,128)S(1)} %broadcast_select_fusion.4), channel_id=1, source_target_pairs={{0,32},{4,36},{8,40},{12,44},{16,48},{20,52},{24,56},{28,60},{32,6... | collective-permute-start | bytes 3145736 | tf_op jit(solution)/shard_map/ppermute | solution.py:35
  298.8 24.9 %collective-permute-start.17 = (f32[4,16,32,128]{3,1,2,0:T(8,128)S(1)}, f32[4,16,32,128]{3,1,2,0:T(8,128)S(1)}, u32[]{:S(2)}, u32[]{:S(2)}) collective-permute-start(f32[4,16,32,128]{3,1,2,0:T(8,128)S(1)} %broadcast_select_fusion.6), channel_id=1, source_target_pairs={{0,4},{4,8},{8,12},{12,16},{16,20},{20,24},{24,28},{28,32},{32,36}... | collective-permute-start | bytes 3145736 | tf_op jit(solution)/shard_map/ppermute | solution.py:35
  336.0 60.7 %all-to-all-start = ((f32[64,16,512]{2,1,0:T(8,128)}), f32[64,16,512]{2,1,0:T(8,128)S(1)}, u32[]{:S(2)}, u32[]{:S(2)}) async-start(f32[64,16,512]{2,1,0:T(8,128)} %stack.41), calls=%async_computation | async-start | bytes 4194304 | tf_op jit(solution)/shard_map/all_to_all | solution.py:159
  (30 other events, 667.5 us)
